TPU v7x, 256 devices: a whole 4x4x8 slice. The times are simulated.
256 devices in a mesh: row: 32 (over z, x), col: 8 (over y, core).
Axes of the slice: x: 4, y: 4, z: 8, core: 2. Of those that a mesh axis runs over, the one named last changes fastest.
Arguments:
- trail_grad: bfloat16 [16384, 16384], P('row', 'col'), may hold values from -6 to 6
- panel_factor: bfloat16 [16384, 1024], P('col'), may hold values from -0.046875 to 0.046875
- cross_factor: bfloat16 [512, 512], replicated, may hold values from -0.25 to 0.25
- diag_factor: bfloat16 [2, 512, 512], replicated, may hold values from -1 to 3, as said below
- diag_inverse: float32 [2, 512, 512], replicated, may hold values from -2 to 2, as said below
- panel_grad: bfloat16 [16384, 1024], P('row'), may hold values from -6 to 6
- cross_grad: bfloat16 [512, 512], replicated, may hold values from -6 to 6
- diag_grad: bfloat16 [2, 512, 512], replicated, may hold values from -6 to 6
Outputs:
- panel_adj: float32 [16384, 1024], P('row', 'col')
- cross_adj: float32 [512, 512], P('col')
- diag_adj: float32 [2, 512, 512], P(None, 'col')
Inputs may be any that keep to these rules, and one draw needn't show every extreme that they name: Each diag_factor[p] is lower triangular with a positive diagonal. diag_inverse[p] is the float32 inverse of diag_factor[p], lower triangular.
All inputs are finite; a program needn't handle non-finite values.
Results may differ from a plain program's by a relative error of at most 0.0003.
Values may be sent and summed in bfloat16 or wider, within the bound.
A program may use at most 128 MiB of HBM per device.

v0:
```python
import jax
import jax.numpy as jnp
from jax import lax
from jax.sharding import Mesh
from jax.sharding import PartitionSpec as P

ROW = ("row_0", "row_1")


def broadcast(x, axis, root):
    return lax.dynamic_index_in_dim(lax.all_gather(x, axis), root, 0, keepdims=False)


def whole_of(x, axes, dim):
    for axis in reversed(axes):
        x = lax.all_gather(x, axis, axis=dim, tiled=True)
    return x


def gathered_total(x, axis):
    blocks = lax.all_gather(x, axis)
    return blocks.sum(axis=0)


def cut_along(x, dim, devices):
    before, after = (x.shape[:dim], x.shape[dim + 1 :])
    return jnp.moveaxis(x.reshape(*before, devices, -1, *after), dim, 0)


def summed_on_arrival(x, axis, dim):
    devices = lax.axis_size(axis)
    blocks = lax.all_to_all(cut_along(x, dim, devices), axis, 0, 0, tiled=True)
    return jnp.sum(blocks, axis=0)


def padded_to(lines, devices):
    spare = -len(lines) % devices
    return jnp.pad(lines, [(0, spare)] + [(0, 0)] * (lines.ndim - 1))


def laid_out(blocks, dim):
    blocks = jnp.moveaxis(blocks, 0, dim)
    lengths = blocks.shape
    return blocks.reshape(*lengths[:dim], lengths[dim] * lengths[dim + 1], *lengths[dim + 2 :])


def copy_for_each(x, axis):
    devices = lax.axis_size(axis)
    return lax.all_to_all(jnp.broadcast_to(x[None], (devices, *x.shape)), axis, 0, 0, tiled=True)


def gather_directly(x, axis, dim):
    return laid_out(copy_for_each(x, axis), dim)


def sum_by_parts(x, axes):
    own = summed_on_arrival(padded_to(x, lax.axis_size(axes)), axes, 0)
    whole = gather_directly(own, axes, 0)
    return whole[: len(x)].reshape(x.shape)


def packed_total(arrays, axis):
    vector, at, finished = (jnp.concatenate([a.reshape(-1) for a in arrays]), 0, [])
    subtotal = sum_by_parts(vector, axis)
    for a in arrays:
        finished.append(subtotal[at : at + a.size].reshape(a.shape))
        at += a.size
    return tuple(finished)


def total_of(x, axes):
    lines = x.reshape(-1, x.shape[-1])
    padded = padded_to(lines, lax.axis_size(axes))
    whole = gather_directly(summed_on_arrival(padded, axes, 0), axes, 0)
    return lax.slice_in_dim(whole, 0, len(lines)).reshape(x.shape)


def halve_lower(matrix):
    size = matrix.shape[0]
    row_ids = lax.broadcasted_iota(jnp.int32, (size, size), 0)
    col_ids = lax.broadcasted_iota(jnp.int32, (size, size), 1)
    return jnp.where(
        col_ids < row_ids,
        matrix,
        jnp.where(col_ids == row_ids, matrix * 0.5, jnp.zeros_like(matrix)),
    )


def inner_rows(left_mat, right_mat):
    return lax.dot_general(
        left_mat, right_mat, (((0,), (0,)), ((), ())), precision=lax.Precision.HIGHEST
    )


def block_adjoint(factor_block, inverse_block, gradient):
    product = inner_rows(factor_block.astype(jnp.float32), gradient)
    halved = halve_lower(product)
    symmetric = halved + halved.T
    inner = inner_rows(inverse_block, symmetric)
    return jnp.dot(inner, inverse_block, precision=lax.Precision.HIGHEST)


def shards(
    trail_grad,
    panel_factor,
    cross_factor,
    diag_factor,
    diag_inverse,
    panel_grad,
    cross_grad,
    diag_grad,
):
    highest = lax.Precision.HIGHEST
    panel_width = cross_factor.shape[0]
    rows_here, cols_here = trail_grad.shape
    stride = lax.axis_size(ROW) // lax.axis_size("col")
    row_id = lax.axis_index(ROW)
    col_id = lax.axis_index("col")
    row_glob = row_id * rows_here + lax.broadcasted_iota(jnp.int32, (rows_here, cols_here), 0)
    col_glob = col_id * cols_here + lax.broadcasted_iota(jnp.int32, (rows_here, cols_here), 1)
    filler = jnp.zeros_like(trail_grad)
    lower_half = jnp.where(
        col_glob < row_glob,
        trail_grad,
        jnp.where(col_glob == row_glob, trail_grad * jnp.bfloat16(0.5), filler),
    )
    own_offset = row_id % stride * rows_here
    own_piece = lax.dynamic_slice_in_dim(panel_factor, own_offset, rows_here, 0)
    factor_rows = broadcast(own_piece, "col", row_id // stride)
    strips = lax.all_to_all(lower_half, "col", split_axis=0, concat_axis=1, tiled=True)
    mirror_block = lax.all_to_all(strips, ROW, split_axis=1, concat_axis=0, tiled=True)
    piece_rows = rows_here // lax.axis_size("col")
    strip_factor = lax.dynamic_slice_in_dim(factor_rows, col_id * piece_rows, piece_rows, 0)
    strip_factor = whole_of(strip_factor, ROW, 0)

    def trailing(first_col, col_count):
        local_cols = panel_factor[:, first_col : first_col + col_count]
        direct_term = jnp.dot(lower_half, local_cols, preferred_element_type=jnp.float32)
        strip_cols = strip_factor[:, first_col : first_col + col_count]
        direct_term = direct_term + lax.dot_general(
            mirror_block, strip_cols, (((0,), (0,)), ((), ())), preferred_element_type=jnp.float32
        )
        direct_term = gathered_total(direct_term, "col")
        return direct_term

    factor_float = factor_rows.astype(jnp.float32)
    factor_zero = factor_float[:, :panel_width]
    factor_one = factor_float[:, panel_width:]
    grads = panel_grad.astype(jnp.float32)
    trail_one = trailing(panel_width, panel_width)
    adj_one = jnp.dot(grads[:, panel_width:] - trail_one, diag_inverse[1], precision=highest)
    row_sums = packed_total(
        (inner_rows(adj_one, factor_one), inner_rows(adj_one, factor_zero)), ROW
    )
    grad_one = diag_grad[1].astype(jnp.float32) - row_sums[0]
    block_one = block_adjoint(diag_factor[1], diag_inverse[1], grad_one)
    trail_zero = trailing(0, panel_width)
    cross_f = cross_factor.astype(jnp.float32)
    rest = grads[:, :panel_width] - trail_zero - jnp.dot(adj_one, cross_f, precision=highest)
    cross_rest = (
        cross_grad.astype(jnp.float32)
        - row_sums[1]
        - jnp.dot(block_one, cross_f, precision=highest)
    )
    adj_zero = jnp.dot(rest, diag_inverse[0], precision=highest)
    cross_adj = jnp.dot(cross_rest, diag_inverse[0], precision=highest)
    zero_sum = total_of(inner_rows(adj_zero, factor_zero), ROW)
    grad_zero = diag_grad[0].astype(jnp.float32) - zero_sum - inner_rows(cross_adj, cross_f)
    block_zero = block_adjoint(diag_factor[0], diag_inverse[0], grad_zero)
    full_panels = jnp.concatenate([adj_zero, adj_one], axis=1)
    out_cols = 2 * panel_width // lax.axis_size("col")
    out_rows = panel_width // lax.axis_size("col")
    panel_part = lax.dynamic_slice_in_dim(full_panels, col_id * out_cols, out_cols, 1)
    cross_part = lax.dynamic_slice_in_dim(cross_adj, col_id * out_rows, out_rows, 0)
    blocks = jnp.stack([block_zero, block_one])
    block_part = lax.dynamic_slice_in_dim(blocks, col_id * out_rows, out_rows, 1)
    return (panel_part, cross_part, block_part)


def solution(mesh):
    split = Mesh(mesh.devices.reshape(8, 4, mesh.shape["col"]), ("row_0", "row_1", "col"))
    return jax.shard_map(
        shards,
        mesh=split,
        in_specs=(P(ROW, "col"), P("col", None), P(), P(), P(), P(ROW, None), P(), P()),
        out_specs=(P(ROW, "col"), P("col", None), P(None, "col", None)),
        check_vma=False,
    )
```

profile of v0, /device:TPU:2, one launch (start us, length us, event | category | flops | bytes accessed | tf_op | source)
XLA Modules:
  0.0 469.4 jit_solution(4517538400826152772)
XLA Ops:
  9.8 55.4 %all-gather.10.cloned.1.call-done = bf16[4096,1024]{1,0:T(8,128)(2,1)} async-done(((bf16[512,1024]{1,0:T(8,128)(2,1)}), bf16[4096,1024]{1,0:T(8,128)(2,1)}) %all-gather.10.cloned.1.call-update) | async-done | bytes 8388624 | tf_op jit(solution)/shard_map/all_gather | solution.py:11
  66.1 13.8 %all-gather.1 = bf16[1,256,1024]{2,1,0:T(8,128)(2,1)} all-gather(bf16[1,64,1024]{2,1,0:T(8,128)(2,1)S(1)} %constant_dynamic-slice_fusion.1), channel_id=3, replica_groups=mesh['row_0'=8,'row_1'=4,'col'=8] {'row_1'}, dimensions={1}, use_global_device_ids=true | all-gather | bytes 655360 | tf_op jit(solution)/shard_map/all_gather | solution.py:16
  81.1 30.5 %all_to_all.60 = bf16[8,64,2048]{2,1,0:T(8,128)(2,1)S(1)} all-to-all(bf16[8,64,2048]{2,1,0:T(8,128)(2,1)S(1)} %bitcast.85), channel_id=1, replica_groups=mesh['row_0'=8,'row_1'=4,'col'=8] {'col'}, dimensions={0} | all-to-all | bytes 4194304 | tf_op jit(solution)/shard_map/all_to_all | solution.py:130
  118.2 63.3 %all_to_all.61 = bf16[64,32,512]{2,0,1:T(8,128)(2,1)S(1)} all-to-all(bf16[64,32,512]{2,0,1:T(8,128)(2,1)S(1)} %copy.20), channel_id=1, replica_groups=mesh['row_0'=8,'row_1'=4,'col'=8] {'row_0','row_1'}, dimensions={1} | all-to-all | bytes 4194304 | tf_op jit(solution)/shard_map/all_to_all | solution.py:131
  184.6 3.9 fusion.11
  192.1 3.9 fusion.8
  199.1 38.5 %all-gather.16.cloned.1.call-done = f32[4096,512]{1,0:T(8,128)} async-done(((f32[512,512]{1,0:T(8,128)}), f32[4096,512]{1,0:T(8,128)}) %all-gather.16.cloned.1.call-update) | async-done | bytes 8388624 | tf_op jit(solution)/shard_map/all_gather | solution.py:21
  237.5 5.5 %reduce_sum.37 = f32[512,512]{1,0:T(8,128)} reduce(f32[8,512,512]{2,1,0:T(8,128)} %bitcast.84, f32[]{:T(128)} %constant.77.clone.1), dimensions={0}, to_apply=%region_1.2 | reduce | flops 1835008 | bytes 9437188 | tf_op jit(solution)/shard_map/reduce_sum | solution.py:22
  243.0 3.7 fusion.15
  257.4 3.6 all_to_all.49
  261.0 10.5 %all-to-all-start.2 = ((f32[32,1,16384]{2,1,0:T(1,128)}), f32[32,1,16384]{2,1,0:T(1,128)}, u32[]{:S(2)}, u32[]{:S(2)}) async-start(f32[32,1,16384]{2,1,0:T(1,128)} %all_to_all.49), calls=%async_computation.2 | async-start | bytes 4194304 | tf_op jit(solution)/shard_map/all_to_all | solution.py:32
  271.5 20.2 %all-gather.14.cloned.1.call-done = f32[4096,512]{1,0:T(8,128)} async-done(((f32[512,512]{1,0:T(8,128)}), f32[4096,512]{1,0:T(8,128)}) %all-gather.14.cloned.1.call-update) | async-done | bytes 8388624 | tf_op jit(solution)/shard_map/all_gather | solution.py:21
  291.8 4.5 reduce_sum.36
  302.6 18.4 %all-to-all-done.2 = f32[32,1,16384]{2,1,0:T(1,128)} async-done(((f32[32,1,16384]{2,1,0:T(1,128)}), f32[32,1,16384]{2,1,0:T(1,128)}, u32[]{:S(2)}, u32[]{:S(2)}) %all-to-all-start.2) | async-done | bytes 2097184 | tf_op jit(solution)/shard_map/all_to_all | solution.py:32
  321.0 6.3 %all-to-all-start.4 = ((f32[32,16,512]{2,1,0:T(8,128)}), f32[32,16,512]{2,1,0:T(8,128)}, u32[]{:S(2)}, u32[]{:S(2)}) async-start(f32[32,16,512]{2,1,0:T(8,128)} %bitcast.89), calls=%async_computation.4 | async-start | bytes 2097152 | tf_op jit(solution)/shard_map/all_to_all | solution.py:32
  330.3 25.2 %all-to-all-done.4 = f32[32,16,512]{2,1,0:T(8,128)} async-done(((f32[32,16,512]{2,1,0:T(8,128)}), f32[32,16,512]{2,1,0:T(8,128)}, u32[]{:S(2)}, u32[]{:S(2)}) %all-to-all-start.4) | async-done | bytes 1048608 | tf_op jit(solution)/shard_map/all_to_all | solution.py:32
  358.7 5.6 %all-to-all-start.3 = ((f32[32,1,16384]{2,1,0:T(1,128)}), f32[32,1,16384]{2,1,0:T(1,128)}, u32[]{:S(2)}, u32[]{:S(2)}) async-start(f32[32,1,16384]{2,1,0:T(1,128)} %broadcast_in_dim.7), calls=%async_computation.3 | async-start | bytes 4194304 | tf_op jit(solution)/shard_map/all_to_all | solution.py:49
  366.5 3.5 reshape.67
  372.2 40.9 %all-to-all-done.3 = f32[32,1,16384]{2,1,0:T(1,128)} async-done(((f32[32,1,16384]{2,1,0:T(1,128)}), f32[32,1,16384]{2,1,0:T(1,128)}, u32[]{:S(2)}, u32[]{:S(2)}) %all-to-all-start.3) | async-done | bytes 2097184 | tf_op jit(solution)/shard_map/all_to_all | solution.py:49
  414.2 6.7 %all-to-all-start.5 = ((f32[32,16,512]{2,1,0:T(8,128)}), f32[32,16,512]{2,1,0:T(8,128)}, u32[]{:S(2)}, u32[]{:S(2)}) async-start(f32[32,16,512]{2,1,0:T(8,128)} %broadcast_in_dim.8), calls=%async_computation.5 | async-start | bytes 2097152 | tf_op jit(solution)/shard_map/all_to_all | solution.py:49
  421.0 8.3 %slice_reduce_fusion = (f32[16,16384]{1,0:T(8,128)}, f32[16,16384]{1,0:T(8,128)S(1)}) fusion(f32[32,1,16384]{2,1,0:T(1,128)} %all-to-all-done.3, f32[16,1,16384]{2,1,0:T(1,128)S(1)} %copy-done.11), kind=kLoop, calls=%fused_computation.23 | loop fusion | flops 262144 | bytes 5242880 | tf_op jit(solution)/shard_map/slice | solution.py:66
  432.9 3.5 fusion.51
  438.9 3.5 fusion.22
  456.2 3.8 fusion.18
  (85 shorter events, 71.8 us)
Async XLA Ops:
  7.2 289.1 %copy-start = (bf16[512,512]{1,0:T(8,128)(2,1)S(1)}, bf16[512,512]{1,0:T(8,128)(2,1)}, u32[]{:S(2)}) copy-start(bf16[512,512]{1,0:T(8,128)(2,1)} %param.10) | copy-start | bytes 1572868
  7.2 58.0 %all-gather.10.cloned.1.call-start = ((), (), s32[]{:S(2)}) async-start(), calls=%async_computation.6 | async-start | bytes 9437184 | tf_op jit(solution)/shard_map/all_gather | solution.py:11
  7.2 72.8 %copy-start.14 = (bf16[512,2048]{1,0:T(8,128)(2,1)S(1)}, bf16[512,2048]{1,0:T(8,128)(2,1)}, u32[]{:S(2)}) copy-start(bf16[512,2048]{1,0:T(8,128)(2,1)} %param.8) | copy-start | bytes 6291460
  9.7 171.8 %all-gather.12.cloned.1.call-start = ((), (), s32[]{:S(2)}) async-start(), calls=%async_computation.7 | async-start | bytes 4718592 | tf_op jit(solution)/shard_map/all_gather | solution.py:16
  79.9 157.6 %all-gather.16.cloned.1.call-start = ((), (), s32[]{:S(2)}) async-start(), calls=%async_computation.9 | async-start | bytes 9437184 | tf_op jit(solution)/shard_map/all_gather | solution.py:21
  81.1 30.5 %copy-start.5 = (bf16[512,2048]{1,0:T(8,128)(2,1)}, bf16[512,2048]{1,0:T(8,128)(2,1)S(1)}, u32[]{:S(2)}) copy-start(bf16[512,2048]{1,0:T(8,128)(2,1)S(1)} %compare_select_fusion.1) | copy-start | bytes 6291460
  181.5 3.0 copy-start.6
  188.4 103.3 %all-gather.14.cloned.1.call-start = ((), (), s32[]{:S(2)}) async-start(), calls=%async_computation.8 | async-start | bytes 9437184 | tf_op jit(solution)/shard_map/all_gather | solution.py:21
  189.0 3.0 copy-start.7
  192.0 4.0 copy-start.15
  199.1 52.2 %copy-start.8 = (bf16[512,1024]{1,0:T(8,128)(2,1)}, bf16[512,1024]{1,0:T(8,128)(2,1)S(1)}, u32[]{:S(2)}) copy-start(bf16[512,1024]{1,0:T(8,128)(2,1)S(1)} %dynamic-slice_bitcast_fusion) | copy-start | bytes 3145732
  253.2 2.8 copy-start.13
  261.0 60.0 %all-to-all-start.2 = ((f32[32,1,16384]{2,1,0:T(1,128)}), f32[32,1,16384]{2,1,0:T(1,128)}, u32[]{:S(2)}, u32[]{:S(2)}) async-start(f32[32,1,16384]{2,1,0:T(1,128)} %all_to_all.49), calls=%async_computation.2 | async-start | bytes 4194304 | tf_op jit(solution)/shard_map/all_to_all | solution.py:32
  296.3 2.4 copy-start.1
  298.7 1.9 copy-start.9
  321.0 34.5 %all-to-all-start.4 = ((f32[32,16,512]{2,1,0:T(8,128)}), f32[32,16,512]{2,1,0:T(8,128)}, u32[]{:S(2)}, u32[]{:S(2)}) async-start(f32[32,16,512]{2,1,0:T(8,128)} %bitcast.89), calls=%async_computation.4 | async-start | bytes 2097152 | tf_op jit(solution)/shard_map/all_to_all | solution.py:32
  358.7 54.4 %all-to-all-start.3 = ((f32[32,1,16384]{2,1,0:T(1,128)}), f32[32,1,16384]{2,1,0:T(1,128)}, u32[]{:S(2)}, u32[]{:S(2)}) async-start(f32[32,1,16384]{2,1,0:T(1,128)} %broadcast_in_dim.7), calls=%async_computation.3 | async-start | bytes 4194304 | tf_op jit(solution)/shard_map/all_to_all | solution.py:49
  370.9 50.1 %copy-start.11 = (f32[16,1,16384]{2,1,0:T(1,128)S(1)}, f32[16,1,16384]{2,1,0:T(1,128)}, u32[]{:S(2)}) copy-start(f32[16,1,16384]{2,1,0:T(1,128)} %reshape.67) | copy-start | bytes 3145732
  414.2 34.6 %all-to-all-start.5 = ((f32[32,16,512]{2,1,0:T(8,128)}), f32[32,16,512]{2,1,0:T(8,128)}, u32[]{:S(2)}, u32[]{:S(2)}) async-start(f32[32,16,512]{2,1,0:T(8,128)} %broadcast_in_dim.8), calls=%async_computation.5 | async-start | bytes 2097152 | tf_op jit(solution)/shard_map/all_to_all | solution.py:49
  432.9 6.1 %copy-start.2 = (f32[2,512,512]{2,1,0:T(8,128)S(1)}, f32[2,512,512]{2,1,0:T(8,128)}, u32[]{:S(2)}) copy-start(f32[2,512,512]{2,1,0:T(8,128)} %param.12) | copy-start | bytes 6291460
  442.4 1.9 copy-start.12
  442.4 1.9 copy-start.17
  448.8 2.8 copy-start.16
  460.0 1.9 copy-start.4
  (2 other events, 2.0 us)
Sparse Core Ops, SparseCore 0:
  9.9 55.2 all-gather.9
  80.0 61.5 all-gather.11
  188.6 48.9 all-gather.15
  239.2 52.4 all-gather.13
where the time goes:
time: 476 us; the launch traced here: 469 us
  waiting for transfers between devices  199 us (42%)
  blocking collectives  108 us (23%)
  matrix products  49.8 us (10%)
  local copies, waits for them, and re-layouts  39.2 us (8%)
  starting transfers between devices  29.9 us (6%)
  other arithmetic  29.7 us (6%)
  between operations  14.5 us (3%)
    all_to_all x1, blocking collectives, shards(): lax.all_to_all(strips, ROW, split_axis=1, concat_axis=0, tiled=True)  63.3 us
    all_gather x2, waiting for transfers between devices, gathered_total(): blocks = lax.all_gather(x, axis)  58.7 us
    all_gather x1, waiting for transfers between devices, broadcast(): lax.all_gather(x, axis)  55.4 us
    all_to_all x2, waiting for transfers between devices, summed_on_arrival(): blocks = lax.all_to_all(cut_along(x, dim, devices), axis, 0, 0, tiled=True)  43.6 us
    all_to_all x2, waiting for transfers between devices, copy_for_each(): lax.all_to_all(jnp.broadcast_to(x[None], (devices, *x.shape)), axis, 0, 0...  40.9 us
    all_to_all x1, blocking collectives, shards(): lax.all_to_all(lower_half, 'col', split_axis=0, concat_axis=1, tiled=True)  30.5 us
    dot_general x8, matrix products, inner_rows(): lax.dot_general(left_mat, right_mat, (((0,), (0,)), ((), ())), precision=...  21.5 us
    all_to_all x2, starting transfers between devices, summed_on_arrival(): blocks = lax.all_to_all(cut_along(x, dim, devices), axis, 0, 0, tiled=True)  16.9 us
  transfers between devices with their start and end apart: 8, of which 6 were waited for; matrix products, arithmetic and copies ran while one was open for 18% of the time, Pallas kernels for 0%

commit v1 on v0

--- a/solution.py
+++ b/solution.py
@@ -127,7 +127,10 @@
     own_offset = row_id % stride * rows_here
     own_piece = lax.dynamic_slice_in_dim(panel_factor, own_offset, rows_here, 0)
     factor_rows = broadcast(own_piece, "col", row_id // stride)
-    strips = lax.all_to_all(lower_half, "col", split_axis=0, concat_axis=1, tiled=True)
+    strips = jnp.concatenate(
+        lax.all_to_all(jnp.stack(jnp.split(lower_half, lax.axis_size("col"), axis=0)), "col", 0, 0),
+        axis=1,
+    )
     mirror_block = lax.all_to_all(strips, ROW, split_axis=1, concat_axis=0, tiled=True)
     piece_rows = rows_here // lax.axis_size("col")
     strip_factor = lax.dynamic_slice_in_dim(factor_rows, col_id * piece_rows, piece_rows, 0)

time: 476 us -> 476 us (level)
  waiting for transfers between devices: 199 us -> 193 us
  local copies, waits for them, and re-layouts: 39.2 us -> 44.9 us
    all_gather x1, waiting for transfers between devices: 55.4 us -> 49.7 us  [broadcast(): lax.all_gather(x, axis)]
    unnamed x37 -> x42, local copies, waits for them, and re-layouts: 1.89 us -> 6.99 us
  transfers between devices with their start and end apart: 8 -> 8, of which waited for: 6 -> 6; matrix products, arithmetic and copies ran while one was open for 18% -> 19% of each run, Pallas kernels for 0% -> 0%
where the time goes in v1:
time: 476 us; the launch traced here: 469 us
  waiting for transfers between devices  193 us (41%)
  blocking collectives  106 us (22%)
  matrix products  49.9 us (10%)
  local copies, waits for them, and re-layouts  44.9 us (9%)
  other arithmetic  31.3 us (7%)
  starting transfers between devices  29.9 us (6%)
  between operations  14.5 us (3%)
    all_to_all x1, blocking collectives, shards(): lax.all_to_all(strips, ROW, split_axis=1, concat_axis=0, tiled=True)  61.2 us
    all_gather x2, waiting for transfers between devices, gathered_total(): blocks = lax.all_gather(x, axis)  58.7 us
    all_gather x1, waiting for transfers between devices, broadcast(): lax.all_gather(x, axis)  49.7 us
    all_to_all x2, waiting for transfers between devices, summed_on_arrival(): blocks = lax.all_to_all(cut_along(x, dim, devices), axis, 0, 0, tiled=True)  43.6 us
    all_to_all x2, waiting for transfers between devices, copy_for_each(): lax.all_to_all(jnp.broadcast_to(x[None], (devices, *x.shape)), axis, 0, 0...  40.9 us
    all_to_all x1, blocking collectives, shards(): lax.all_to_all(jnp.stack(jnp.split(lower_half, lax.axis_size('col'), axis...  31 us
    dot_general x8, matrix products, inner_rows(): lax.dot_general(left_mat, right_mat, (((0,), (0,)), ((), ())), precision=...  21.6 us
    all_to_all x2, starting transfers between devices, summed_on_arrival(): blocks = lax.all_to_all(cut_along(x, dim, devices), axis, 0, 0, tiled=True)  16.9 us
  transfers between devices with their start and end apart: 8, of which 6 were waited for; matrix products, arithmetic and copies ran while one was open for 19% of the time, Pallas kernels for 0%

profile of v1, /device:TPU:2, one launch (start us, length us, event | category | flops | bytes accessed | tf_op | source)
XLA Modules:
  0.0 469.4 jit_solution(11806304994284824435)
XLA Ops:
  15.4 49.7 %all-gather.10.cloned.1.call-done = bf16[4096,1024]{1,0:T(8,128)(2,1)} async-done(((bf16[512,1024]{1,0:T(8,128)(2,1)}), bf16[4096,1024]{1,0:T(8,128)(2,1)}) %all-gather.10.cloned.1.call-update) | async-done | bytes 8388624 | tf_op jit(solution)/shard_map/all_gather | solution.py:11
  66.1 13.8 %all-gather.1 = bf16[1,256,1024]{2,1,0:T(8,128)(2,1)} all-gather(bf16[1,64,1024]{2,1,0:T(8,128)(2,1)S(1)} %constant_dynamic-slice_fusion.1), channel_id=3, replica_groups=mesh['row_0'=8,'row_1'=4,'col'=8] {'row_1'}, dimensions={1}, use_global_device_ids=true | all-gather | bytes 655360 | tf_op jit(solution)/shard_map/all_gather | solution.py:16
  82.8 31.0 %all_to_all.49 = bf16[8,64,2048]{2,1,0:T(8,128)(2,1)S(1)} all-to-all(bf16[8,64,2048]{2,1,0:T(8,128)(2,1)} %fusion.65), channel_id=1, replica_groups=mesh['row_0'=8,'row_1'=4,'col'=8] {'col'}, dimensions={0} | all-to-all | bytes 4194304 | tf_op jit(solution)/shard_map/all_to_all | solution.py:131
  120.4 61.2 %all_to_all.50 = bf16[64,32,512]{2,0,1:T(8,128)(2,1)S(1)} all-to-all(bf16[64,32,512]{2,0,1:T(8,128)(2,1)S(1)} %copy.20), channel_id=1, replica_groups=mesh['row_0'=8,'row_1'=4,'col'=8] {'row_0','row_1'}, dimensions={1} | all-to-all | bytes 4194304 | tf_op jit(solution)/shard_map/all_to_all | solution.py:134
  184.6 3.9 fusion.11
  192.1 3.9 fusion.8
  199.1 38.5 %all-gather.16.cloned.1.call-done = f32[4096,512]{1,0:T(8,128)} async-done(((f32[512,512]{1,0:T(8,128)}), f32[4096,512]{1,0:T(8,128)}) %all-gather.16.cloned.1.call-update) | async-done | bytes 8388624 | tf_op jit(solution)/shard_map/all_gather | solution.py:21
  237.5 5.5 %reduce_sum.37 = f32[512,512]{1,0:T(8,128)} reduce(f32[8,512,512]{2,1,0:T(8,128)} %bitcast.115, f32[]{:T(128)} %constant.77.clone.1), dimensions={0}, to_apply=%region_1.2 | reduce | flops 1835008 | bytes 9437188 | tf_op jit(solution)/shard_map/reduce_sum | solution.py:22
  243.0 3.7 fusion.15
  257.4 3.6 all_to_all.38
  261.0 10.6 %all-to-all-start.2 = ((f32[32,1,16384]{2,1,0:T(1,128)}), f32[32,1,16384]{2,1,0:T(1,128)}, u32[]{:S(2)}, u32[]{:S(2)}) async-start(f32[32,1,16384]{2,1,0:T(1,128)} %all_to_all.38), calls=%async_computation.2 | async-start | bytes 4194304 | tf_op jit(solution)/shard_map/all_to_all | solution.py:32
  271.5 20.3 %all-gather.14.cloned.1.call-done = f32[4096,512]{1,0:T(8,128)} async-done(((f32[512,512]{1,0:T(8,128)}), f32[4096,512]{1,0:T(8,128)}) %all-gather.14.cloned.1.call-update) | async-done | bytes 8388624 | tf_op jit(solution)/shard_map/all_gather | solution.py:21
  291.8 4.5 reduce_sum.36
  302.6 18.4 %all-to-all-done.2 = f32[32,1,16384]{2,1,0:T(1,128)} async-done(((f32[32,1,16384]{2,1,0:T(1,128)}), f32[32,1,16384]{2,1,0:T(1,128)}, u32[]{:S(2)}, u32[]{:S(2)}) %all-to-all-start.2) | async-done | bytes 2097184 | tf_op jit(solution)/shard_map/all_to_all | solution.py:32
  321.0 6.3 %all-to-all-start.4 = ((f32[32,16,512]{2,1,0:T(8,128)}), f32[32,16,512]{2,1,0:T(8,128)}, u32[]{:S(2)}, u32[]{:S(2)}) async-start(f32[32,16,512]{2,1,0:T(8,128)} %bitcast.119), calls=%async_computation.4 | async-start | bytes 2097152 | tf_op jit(solution)/shard_map/all_to_all | solution.py:32
  330.3 25.2 %all-to-all-done.4 = f32[32,16,512]{2,1,0:T(8,128)} async-done(((f32[32,16,512]{2,1,0:T(8,128)}), f32[32,16,512]{2,1,0:T(8,128)}, u32[]{:S(2)}, u32[]{:S(2)}) %all-to-all-start.4) | async-done | bytes 1048608 | tf_op jit(solution)/shard_map/all_to_all | solution.py:32
  358.7 5.6 %all-to-all-start.3 = ((f32[32,1,16384]{2,1,0:T(1,128)}), f32[32,1,16384]{2,1,0:T(1,128)}, u32[]{:S(2)}, u32[]{:S(2)}) async-start(f32[32,1,16384]{2,1,0:T(1,128)} %broadcast_in_dim.7), calls=%async_computation.3 | async-start | bytes 4194304 | tf_op jit(solution)/shard_map/all_to_all | solution.py:49
  366.5 3.5 reshape.69
  372.2 40.9 %all-to-all-done.3 = f32[32,1,16384]{2,1,0:T(1,128)} async-done(((f32[32,1,16384]{2,1,0:T(1,128)}), f32[32,1,16384]{2,1,0:T(1,128)}, u32[]{:S(2)}, u32[]{:S(2)}) %all-to-all-start.3) | async-done | bytes 2097184 | tf_op jit(solution)/shard_map/all_to_all | solution.py:49
  414.2 6.7 %all-to-all-start.5 = ((f32[32,16,512]{2,1,0:T(8,128)}), f32[32,16,512]{2,1,0:T(8,128)}, u32[]{:S(2)}, u32[]{:S(2)}) async-start(f32[32,16,512]{2,1,0:T(8,128)} %broadcast_in_dim.8), calls=%async_computation.5 | async-start | bytes 2097152 | tf_op jit(solution)/shard_map/all_to_all | solution.py:49
  420.9 8.3 %slice_reduce_fusion = (f32[16,16384]{1,0:T(8,128)}, f32[16,16384]{1,0:T(8,128)S(1)}) fusion(f32[32,1,16384]{2,1,0:T(1,128)} %all-to-all-done.3, f32[16,1,16384]{2,1,0:T(1,128)S(1)} %copy-done.11), kind=kLoop, calls=%fused_computation.23 | loop fusion | flops 262144 | bytes 5242880 | tf_op jit(solution)/shard_map/slice | solution.py:66
  432.9 3.5 fusion.51
  438.9 3.5 fusion.22
  456.2 3.8 fusion.18
  (91 shorter events, 79.2 us)
Async XLA Ops:
  7.2 289.1 %copy-start = (bf16[512,512]{1,0:T(8,128)(2,1)S(1)}, bf16[512,512]{1,0:T(8,128)(2,1)}, u32[]{:S(2)}) copy-start(bf16[512,512]{1,0:T(8,128)(2,1)} %param.10) | copy-start | bytes 1572868
  7.2 58.0 %all-gather.10.cloned.1.call-start = ((), (), s32[]{:S(2)}) async-start(), calls=%async_computation.6 | async-start | bytes 9437184 | tf_op jit(solution)/shard_map/all_gather | solution.py:11
  9.7 171.8 %all-gather.12.cloned.1.call-start = ((), (), s32[]{:S(2)}) async-start(), calls=%async_computation.7 | async-start | bytes 4718592 | tf_op jit(solution)/shard_map/all_gather | solution.py:16
  12.5 69.6 %copy-start.5 = (bf16[512,2048]{1,0:T(8,128)(2,1)}, bf16[512,2048]{1,0:T(8,128)(2,1)S(1)}, u32[]{:S(2)}) copy-start(bf16[512,2048]{1,0:T(8,128)(2,1)S(1)} %compare_select_fusion.1) | copy-start | bytes 6291460
  79.9 157.6 %all-gather.16.cloned.1.call-start = ((), (), s32[]{:S(2)}) async-start(), calls=%async_computation.9 | async-start | bytes 9437184 | tf_op jit(solution)/shard_map/all_gather | solution.py:21
  181.5 3.0 copy-start.6
  188.5 103.3 %all-gather.14.cloned.1.call-start = ((), (), s32[]{:S(2)}) async-start(), calls=%async_computation.8 | async-start | bytes 9437184 | tf_op jit(solution)/shard_map/all_gather | solution.py:21
  189.0 3.0 copy-start.7
  192.1 4.0 copy-start.14
  199.1 52.1 %copy-start.8 = (bf16[512,1024]{1,0:T(8,128)(2,1)}, bf16[512,1024]{1,0:T(8,128)(2,1)S(1)}, u32[]{:S(2)}) copy-start(bf16[512,1024]{1,0:T(8,128)(2,1)S(1)} %dynamic-slice_bitcast_fusion) | copy-start | bytes 3145732
  253.2 2.8 copy-start.13
  261.0 60.0 %all-to-all-start.2 = ((f32[32,1,16384]{2,1,0:T(1,128)}), f32[32,1,16384]{2,1,0:T(1,128)}, u32[]{:S(2)}, u32[]{:S(2)}) async-start(f32[32,1,16384]{2,1,0:T(1,128)} %all_to_all.38), calls=%async_computation.2 | async-start | bytes 4194304 | tf_op jit(solution)/shard_map/all_to_all | solution.py:32
  296.3 2.4 copy-start.1
  298.7 1.9 copy-start.9
  321.0 34.5 %all-to-all-start.4 = ((f32[32,16,512]{2,1,0:T(8,128)}), f32[32,16,512]{2,1,0:T(8,128)}, u32[]{:S(2)}, u32[]{:S(2)}) async-start(f32[32,16,512]{2,1,0:T(8,128)} %bitcast.119), calls=%async_computation.4 | async-start | bytes 2097152 | tf_op jit(solution)/shard_map/all_to_all | solution.py:32
  358.7 54.4 %all-to-all-start.3 = ((f32[32,1,16384]{2,1,0:T(1,128)}), f32[32,1,16384]{2,1,0:T(1,128)}, u32[]{:S(2)}, u32[]{:S(2)}) async-start(f32[32,1,16384]{2,1,0:T(1,128)} %broadcast_in_dim.7), calls=%async_computation.3 | async-start | bytes 4194304 | tf_op jit(solution)/shard_map/all_to_all | solution.py:49
  370.8 50.1 %copy-start.11 = (f32[16,1,16384]{2,1,0:T(1,128)S(1)}, f32[16,1,16384]{2,1,0:T(1,128)}, u32[]{:S(2)}) copy-start(f32[16,1,16384]{2,1,0:T(1,128)} %reshape.69) | copy-start | bytes 3145732
  414.2 34.6 %all-to-all-start.5 = ((f32[32,16,512]{2,1,0:T(8,128)}), f32[32,16,512]{2,1,0:T(8,128)}, u32[]{:S(2)}, u32[]{:S(2)}) async-start(f32[32,16,512]{2,1,0:T(8,128)} %broadcast_in_dim.8), calls=%async_computation.5 | async-start | bytes 2097152 | tf_op jit(solution)/shard_map/all_to_all | solution.py:49
  432.9 6.1 %copy-start.2 = (f32[2,512,512]{2,1,0:T(8,128)S(1)}, f32[2,512,512]{2,1,0:T(8,128)}, u32[]{:S(2)}) copy-start(f32[2,512,512]{2,1,0:T(8,128)} %param.12) | copy-start | bytes 6291460
  442.4 1.9 copy-start.12
  442.4 1.9 copy-start.16
  444.3 1.0 copy-start.3
  448.9 2.8 copy-start.15
  460.0 1.9 copy-start.4
  (1 other events, 1.0 us)
Sparse Core Ops, SparseCore 0:
  9.9 55.2 all-gather.9
  80.0 56.9 all-gather.11
  188.6 48.9 all-gather.15
  239.3 52.4 all-gather.13
